TPU v7x, 512 devices: a whole 4x8x8 slice. The times are simulated.
512 devices in a mesh: req: 8 (over y), seq: 8 (over x, core), tp: 8 (over z).
Axes of the slice: x: 4, y: 8, z: 8, core: 2. Of those that a mesh axis runs over, the one named last changes fastest.
Arguments:
- tokens: bfloat16 [2048, 1024], P(('req', 'seq', 'tp')), may hold values from -3 to 3
- w_qkv: bfloat16 [1024, 3, 1024], P(None, None, 'tp'), may hold values from -0.1875 to 0.1875
- w_out: bfloat16 [1024, 1024], P('tp'), may hold values from -0.75 to 0.75
- variate_bias: float32 [2, 16], P(None, 'tp'), may hold values from -2 to 2
- attn_gain: float32 [1024], replicated, may hold values from 0.25 to 1.75
- ffn_gain: float32 [1024], replicated, may hold values from 0.25 to 1.75
- gate_up: bfloat16 [1024, 64, 128], P(None, ('seq', 'tp')), may hold values from -0.1875 to 0.1875
- w_down: bfloat16 [64, 64, 1024], P(('seq', 'tp')), may hold values from -0.09375 to 0.09375
- cache_keys: bfloat16 [1536, 256, 1024], P(('req', 'seq'), None, 'tp'), may hold values from -360 to 360
- cache_values: bfloat16 [1536, 256, 1024], P(('req', 'seq'), None, 'tp'), may hold values from -6 to 6
- cache_variate: int32 [1536, 256], P(('req', 'seq')), may hold values from 0 to 3
- new_variate: int32 [512, 4], P('req'), may hold values from 0 to 3
- piece_slot: int32 [512, 64], P('req'), may hold values from -1 to 191, as said below
- cache_len: int32 [512], P('req'), may hold values from 1 to 16384, as said below
Outputs:
- layer_out: bfloat16 [2048, 1024], P(('req', 'seq', 'tp'))
Inputs may be any that keep to these rules, and one draw needn't show every extreme that they name: `cache_len`: in each aligned block of 64 requests exactly one request has the most cached positions. `piece_slot`: entry p of request r is the slot within its group that holds cache positions p * 256 to p * 256 + 255; it is -1 exactly when p * 256 >= cache_len[r]; no slot of a group holds two pieces; slots that hold no piece are never read.
All inputs are finite; a program needn't handle non-finite values.
Results may differ from a plain program's by a relative error of at most 0.022.
Values may be sent and summed in bfloat16 or wider, within the bound.
No kernel may reach another device: no remote copies, remote signals or barrier semaphores. Data moves between devices by JAX's collectives and lax.ppermute only.
A program may use at most 64 MiB of HBM per device.

v0:
```python
import math
import jax
import jax.numpy as jnp
from jax import lax
from jax.sharding import PartitionSpec as P

HD = 64
EPSILON = 1e-05
MASKED_SCORE = -1e30


def joined(value, axis, combine):
    everything = jax.tree.map(lambda part: lax.all_gather(part, axis), value)
    first = jax.tree.map(lambda part: part[0], everything)

    def step(k, so_far):
        return combine(so_far, jax.tree.map(lambda part: part[k], everything))

    return lax.fori_loop(1, lax.axis_size(axis), step, first)


def rms_scale(rows, gain):
    rows32 = rows.astype(jnp.float32)
    mean_sq = jnp.mean(rows32 * rows32, axis=-1, keepdims=True)
    return (rows32 * lax.rsqrt(mean_sq + EPSILON) * gain).astype(jnp.bfloat16)


def rotate(vectors, positions):
    half_size = vectors.shape[-1] // 2
    inv_freq = 10000.0 ** (-jnp.arange(half_size, dtype=jnp.float32) / half_size)
    angles = positions[:, None] * inv_freq[None, :]
    cosine = jnp.cos(angles)[:, None, :]
    sine_part = jnp.sin(angles)[:, None, :]
    earlier = vectors[..., :half_size]
    latter = vectors[..., half_size:]
    return jnp.concatenate(
        [earlier * cosine - latter * sine_part, latter * cosine + earlier * sine_part], axis=-1
    )


def row_positions(lengths, step_count):
    offsets = jnp.arange(step_count, dtype=jnp.int32)
    return (lengths[:, None] + offsets[None, :]).reshape(-1).astype(jnp.float32)


def split_heads(projected, positions, head_size):
    row_count = projected.shape[0]
    parts = projected.reshape(row_count, 3, -1, head_size)
    queries = rotate(parts[:, 0], positions).astype(jnp.bfloat16)
    keys_new = rotate(parts[:, 1], positions).astype(jnp.bfloat16)
    values_new = parts[:, 2].astype(jnp.bfloat16)
    return (queries, keys_new, values_new)


def cache_partials(
    queries,
    cache_keys,
    cache_values,
    cache_variate,
    new_variate,
    piece_slot,
    cache_len,
    variate_bias,
    score_scale,
):
    slot_count, piece_len, _ = cache_keys.shape
    requests, step_count, heads, head_size = queries.shape
    max_pieces = piece_slot.shape[1]
    slot_ids = lax.axis_index("seq") * slot_count + jnp.arange(slot_count, dtype=jnp.int32)
    matches = piece_slot[None, :, :] == slot_ids[:, None, None]
    owners = jnp.any(matches, axis=2)
    piece_index = jnp.sum(
        jnp.where(matches, jnp.arange(max_pieces, dtype=jnp.int32)[None, None, :], 0), axis=(1, 2)
    )
    owner_len = jnp.sum(jnp.where(owners, cache_len[None, :], 0), axis=1)
    positions_in = (
        piece_index[:, None] * piece_len + jnp.arange(piece_len, dtype=jnp.int32)[None, :]
    )
    is_valid = positions_in < owner_len[:, None]
    picker = owners.astype(jnp.bfloat16)
    slot_query = jnp.dot(
        picker, queries.reshape(requests, -1), preferred_element_type=jnp.float32
    ).astype(jnp.bfloat16)
    slot_query = slot_query.reshape(slot_count, step_count, heads, head_size)
    slot_variate = jnp.sum(jnp.where(owners[:, :, None], new_variate[None], 0), axis=1)
    same_var = slot_variate[:, :, None] == cache_variate[:, None, :]
    bias_terms = jnp.where(
        same_var[:, None],
        variate_bias[0][None, :, None, None],
        variate_bias[1][None, :, None, None],
    )
    key_rows = cache_keys.reshape(slot_count, piece_len, heads, head_size)
    value_rows = cache_values.reshape(slot_count, piece_len, heads, head_size)
    scores = (
        jnp.einsum("sthd,slhd->shtl", slot_query, key_rows, preferred_element_type=jnp.float32)
        * score_scale
        + bias_terms
    )
    scores = jnp.where(is_valid[:, None, None, :], scores, MASKED_SCORE)
    slot_top = jnp.max(scores, axis=3)
    weights = jnp.where(is_valid[:, None, None, :], jnp.exp(scores - slot_top[..., None]), 0.0)
    slot_total = jnp.sum(weights, axis=3)
    slot_out = jnp.einsum(
        "shtl,slhd->shtd",
        weights.astype(jnp.bfloat16),
        value_rows,
        preferred_element_type=jnp.float32,
    )
    top_cache = jnp.max(
        jnp.where(owners[:, :, None, None], slot_top[:, None], MASKED_SCORE), axis=0
    )
    top_at = jnp.sum(jnp.where(owners[:, :, None, None], top_cache[None], 0.0), axis=1)
    factor = jnp.exp(slot_top - top_at)
    owner_f = owners.astype(jnp.float32)
    cache_total = jnp.einsum(
        "sr,sht->rht", owner_f, slot_total * factor, precision=lax.Precision.HIGHEST
    )
    cache_out = jnp.einsum(
        "sr,shtd->rhtd", owner_f, slot_out * factor[..., None], precision=lax.Precision.HIGHEST
    )
    return (top_cache, cache_total, cache_out)


def merge_pair(earlier, latter):
    joint_top = jnp.maximum(earlier[0], latter[0])
    left_scale = jnp.exp(earlier[0] - joint_top)
    right_scale = jnp.exp(latter[0] - joint_top)
    joint_total = earlier[1] * left_scale + latter[1] * right_scale
    joint_out = earlier[2] * left_scale[..., None] + latter[2] * right_scale[..., None]
    return (joint_top, joint_total, joint_out)


def finish(
    top_cache,
    cache_total,
    cache_out,
    queries,
    keys_new,
    values_new,
    new_variate,
    variate_bias,
    score_scale,
):
    step_count = new_variate.shape[1]
    new_scores = (
        jnp.einsum("rthd,ruhd->rhtu", queries, keys_new, preferred_element_type=jnp.float32)
        * score_scale
    )
    same_var = new_variate[:, :, None] == new_variate[:, None, :]
    new_scores = new_scores + jnp.where(
        same_var[:, None],
        variate_bias[0][None, :, None, None],
        variate_bias[1][None, :, None, None],
    )
    step_ids = jnp.arange(step_count, dtype=jnp.int32)
    causal = step_ids[:, None] >= step_ids[None, :]
    new_scores = jnp.where(causal[None, None], new_scores, MASKED_SCORE)
    row_top = jnp.maximum(top_cache, jnp.max(new_scores, axis=3))
    new_weights = jnp.where(causal[None, None], jnp.exp(new_scores - row_top[..., None]), 0.0)
    carried = jnp.exp(top_cache - row_top)
    row_total = cache_total * carried + jnp.sum(new_weights, axis=3)
    mixed_out = cache_out * carried[..., None] + jnp.einsum(
        "rhtu,ruhd->rhtd",
        new_weights.astype(jnp.bfloat16),
        values_new,
        preferred_element_type=jnp.float32,
    )
    attended = mixed_out / row_total[..., None]
    requests, heads, _, head_size = attended.shape
    return (
        jnp.transpose(attended, (0, 2, 1, 3))
        .reshape(requests * step_count, heads * head_size)
        .astype(jnp.bfloat16)
    )


def make_expand(gate_blocks, unit_block, row_block):
    block_count = gate_blocks.shape[1]
    expanded = jnp.einsum("nd,dbu->nbu", row_block, gate_blocks, preferred_element_type=jnp.float32)
    gate_part = expanded[:, :, :unit_block]
    up_part = expanded[:, :, unit_block:]
    return (
        (jax.nn.silu(gate_part) * up_part)
        .astype(jnp.bfloat16)
        .reshape(row_block.shape[0], block_count * unit_block)
    )


def on_device(
    tokens,
    w_qkv,
    w_out,
    variate_bias,
    attn_gain,
    ffn_gain,
    gate_up,
    w_down,
    cache_keys,
    cache_values,
    cache_variate,
    new_variate,
    piece_slot,
    cache_len,
):
    row_count = tokens.shape[0]
    requests, step_count = new_variate.shape
    score_scale = 1.0 / math.sqrt(HD)
    normed = rms_scale(tokens, attn_gain)
    qkv_width = w_qkv.shape[2]
    flat_qkv = w_qkv.reshape(w_qkv.shape[0], 3 * qkv_width)
    projected = jnp.dot(
        lax.all_gather(normed, ("seq", "tp"), axis=0, tiled=True),
        flat_qkv,
        preferred_element_type=jnp.float32,
    )
    queries, keys_new, values_new = split_heads(projected, row_positions(cache_len, step_count), HD)
    shape_four = (requests, step_count, qkv_width // HD, HD)
    queries = queries.reshape(shape_four)
    keys_new = keys_new.reshape(shape_four)
    values_new = values_new.reshape(shape_four)
    top_cache, cache_total, cache_out = cache_partials(
        queries,
        cache_keys,
        cache_values,
        cache_variate,
        new_variate,
        piece_slot,
        cache_len,
        variate_bias,
        score_scale,
    )
    top_cache, cache_total, cache_out = joined(
        (top_cache, cache_total, cache_out), "seq", merge_pair
    )
    attended = finish(
        top_cache,
        cache_total,
        cache_out,
        queries,
        keys_new,
        values_new,
        new_variate,
        variate_bias,
        score_scale,
    )
    seq_base = lax.axis_index("seq") * (row_count * lax.axis_size("tp"))
    picked = lax.dynamic_slice_in_dim(attended, seq_base, row_count * lax.axis_size("tp"), 0)
    attn_rows_sum = lax.psum_scatter(
        jnp.dot(picked, w_out, preferred_element_type=jnp.float32).astype(jnp.bfloat16),
        "tp",
        scatter_dimension=0,
        tiled=True,
    ).astype(jnp.float32)
    mid = tokens.astype(jnp.float32) + attn_rows_sum
    normed_mid = rms_scale(mid, ffn_gain)
    unit_block = w_down.shape[1]
    model_width = w_down.shape[2]
    hidden = make_expand(
        gate_up, unit_block, lax.all_gather(normed_mid, ("seq", "tp"), axis=0, tiled=True)
    )
    flat_down = w_down.reshape(w_down.shape[0] * unit_block, model_width)
    picked = hidden
    ffn_rows_sum = lax.psum_scatter(
        jnp.dot(picked, flat_down, preferred_element_type=jnp.float32),
        ("seq", "tp"),
        scatter_dimension=0,
        tiled=True,
    )
    return (mid + ffn_rows_sum).astype(jnp.bfloat16)


def solution(mesh):
    in_specs = (
        P(("req", "seq", "tp"), None),
        P(None, None, "tp"),
        P("tp", None),
        P(None, "tp"),
        P(),
        P(),
        P(None, ("seq", "tp"), None),
        P(("seq", "tp"), None, None),
        P(("req", "seq"), None, "tp"),
        P(("req", "seq"), None, "tp"),
        P(("req", "seq"), None),
        P("req", None),
        P("req", None),
        P("req"),
    )
    out_specs = P(("req", "seq", "tp"), None)
    return jax.shard_map(
        on_device, mesh=mesh, in_specs=in_specs, out_specs=out_specs, check_vma=False
    )
```

profile of v0, /device:TPU:8, one launch (start us, length us, event | category | flops | bytes accessed | tf_op | source)
XLA Modules:
  0.0 463.1 jit_solution(17933760203444792327)
XLA Ops:
  6.6 1.4 fusion.9
  8.0 1.3 compare_reduce_fusion
  10.8 1.3 slice_bitcast_fusion.3
  12.8 1.3 select_reduce_fusion.3
  16.5 55.1 %all-gather.3 = bf16[64,4,1024]{2,1,0:T(4,128)(2,1)S(1)} all-gather(bf16[1,4,1024]{2,1,0:T(4,128)(2,1)S(1)} %fusion.39), channel_id=1, replica_groups=mesh['req'=8,'seq'=8,'tp'=8] {'seq','tp'}, dimensions={0}, use_global_device_ids=true | all-gather | bytes 532480 | tf_op jit(solution)/shard_map/all_gather | solution.py:212
  76.4 1.7 fusion.47
  78.3 1.2 fusion.20
  80.5 1.5 convolution_multiply_fusion.1
  82.0 1.0 fusion.22
  85.9 13.5 %all-gather = f32[512,2,4]{2,1,0:T(2,128)S(1)} all-gather(f32[64,2,4]{2,1,0:T(2,128)S(1)} %copy.150), channel_id=2, replica_groups=mesh['req'=8,'seq'=8,'tp'=8] {'seq'}, dimensions={0}, use_global_device_ids=true | all-gather | bytes 18432 | tf_op jit(solution)/shard_map/all_gather | solution.py:13
  99.7 13.6 %all-gather.1 = f32[512,2,4]{2,1,0:T(2,128)S(1)} all-gather(f32[64,2,4]{2,1,0:T(2,128)S(1)} %copy.153), channel_id=3, replica_groups=mesh['req'=8,'seq'=8,'tp'=8] {'seq'}, dimensions={0}, use_global_device_ids=true | all-gather | bytes 18432 | tf_op jit(solution)/shard_map/all_gather | solution.py:13
  114.9 14.4 %while.19 = (s32[]{:T(128)}, f32[64,2,4]{0,2,1:T(4,128)S(1)}, f32[64,2,4]{0,2,1:T(4,128)S(1)}, f32[64,2,4,64]{3,2,1,0:T(4,128)S(1)}, f32[8,64,2,4]{1,3,2,0:T(4,1...) while((s32[]{:T(128)}, f32[64,2,4]{0,2,1:T(4,128)S(1)}, ...), condition=%wide.region_10.11_spmd, body=%wide.region_9.10_spmd.sunk | while | flops 101381 | bytes 684175 | solution.py:19
  115.2 1.0 constant_dynamic-slice_fusion.2
  117.3 1.0 constant_dynamic-slice_fusion.2
  119.4 1.0 constant_dynamic-slice_fusion.2
  123.5 1.0 constant_dynamic-slice_fusion.2
  125.5 1.0 constant_dynamic-slice_fusion.2
  131.5 1.3 dynamic-slice
  133.4 74.0 %all-reduce.5.cloned.1.call-done = bf16[32,1024]{1,0:T(8,128)(2,1)} async-done(((bf16[32,1024]{1,0:T(8,128)(2,1)}), bf16[32,1024]{1,0:T(8,128)(2,1)}) %all-reduce.5.cloned.1.call-update) | async-done | bytes 65552
  209.0 48.0 %all-gather.4 = bf16[64,4,1024]{2,1,0:T(4,128)(2,1)S(1)} all-gather(bf16[1,4,1024]{2,1,0:T(4,128)(2,1)S(1)} %fusion.38), channel_id=1, replica_groups=mesh['req'=8,'seq'=8,'tp'=8] {'seq','tp'}, dimensions={0}, use_global_device_ids=true | all-gather | bytes 532480 | tf_op jit(solution)/shard_map/all_gather | solution.py:259
  257.5 1.4 fusion.13
  258.9 1.3 dynamic-slice.2
  260.8 194.3 %all-reduce.7.cloned.1.call-done = f32[256,1024]{1,0:T(8,128)} async-done(((f32[256,1024]{1,0:T(8,128)}), f32[256,1024]{1,0:T(8,128)}) %all-reduce.7.cloned.1.call-update) | async-done | bytes 1048592
  455.2 1.4 fusion.34
  (142 shorter events, 28.5 us)
Async XLA Ops:
  6.5 124.0 %copy-start = (bf16[128,1024]{1,0:T(8,128)(2,1)S(1)}, bf16[128,1024]{1,0:T(8,128)(2,1)}, u32[]{:S(2)}) copy-start(bf16[128,1024]{1,0:T(8,128)(2,1)} %param.18) | copy-start | bytes 786436
  6.5 65.1 %copy-start.4 = (bf16[1024,3,128]{2,0,1:T(8,128)(2,1)S(1)}, bf16[1024,3,128]{2,0,1:T(8,128)(2,1)}, u32[]{:S(2)}) copy-start(bf16[1024,3,128]{2,0,1:T(8,128)(2,1)} %param.17) | copy-start | bytes 2359300
  6.5 107.2 %all-gather.7.cloned.1.call-start = ((), (), s32[]{:S(2)}) async-start(), calls=%async_computation | async-start | bytes 2359296 | tf_op jit(solution)/shard_map/all_gather | solution.py:13
  72.0 2.6 copy-start.1
  72.4 0.8 copy-start.3
  74.5 0.7 copy-start.16
  74.6 0.7 copy-start.17
  74.6 0.8 copy-start.12
  75.3 4.4 copy-start.2
  75.4 2.6 copy-start.10
  79.7 0.7 copy-start.11
  80.5 4.1 copy-start.8
  80.5 4.2 copy-start.7
  83.1 124.3 %all-reduce.5.cloned.1.call-start = ((), (), s32[]{:S(2)}) async-start(), calls=%async_computation.1 | async-start | bytes 131072
  85.5 28.2 %copy-start.13 = (s32[64,4]{0,1:T(4,128)S(1)}, s32[64,4]{0,1:T(4,128)}, u32[]{:S(2)}) copy-start(s32[64,4]{0,1:T(4,128)} %param.27) | copy-start | bytes 3076
  85.5 28.2 %copy-start.14 = (f32[2]{0:T(128)S(1)}, f32[2]{0:T(128)}, u32[]{:S(2)}) copy-start(f32[2]{0:T(128)} %get-tuple-element.258) | copy-start | bytes 28
  129.9 77.5 %copy-start.6 = (bf16[4,1024]{1,0:T(4,128)(2,1)S(1)}, bf16[4,1024]{1,0:T(4,128)(2,1)}, u32[]{:S(2)}) copy-start(bf16[4,1024]{1,0:T(4,128)(2,1)} %param.16) | copy-start | bytes 24580
  129.9 78.3 %copy-start.15 = (f32[1024]{0:T(1024)S(1)}, f32[1024]{0:T(1024)}, u32[]{:S(2)}) copy-start(f32[1024]{0:T(1024)} %param.21) | copy-start | bytes 12292
  130.3 126.9 %copy-start.5 = (bf16[1024,1,128]{2,0,1:T(8,128)(2,1)S(1)}, bf16[1024,1,128]{2,0,1:T(8,128)(2,1)}, u32[]{:S(2)}) copy-start(bf16[1024,1,128]{2,0,1:T(8,128)(2,1)} %param.22) | copy-start | bytes 786436
  130.4 127.1 %copy-start.9 = (bf16[1,64,1024]{2,1,0:T(8,128)(2,1)S(1)}, bf16[1,64,1024]{2,1,0:T(8,128)(2,1)}, u32[]{:S(2)}) copy-start(bf16[1,64,1024]{2,1,0:T(8,128)(2,1)} %param.23) | copy-start | bytes 393220
  131.4 323.8 %all-reduce.7.cloned.1.call-start = ((), (), s32[]{:S(2)}) async-start(), calls=%async_computation.2 | async-start | bytes 2097152
Sparse Core Ops, SparseCore 0:
  83.2 27.9 all-gather.6
  131.5 75.8 all-reduce.4
  259.0 196.1 all-reduce.6
where the time goes:
time: 464 us; the launch traced here: 463 us
  waiting for transfers between devices  268 us (58%)
  blocking collectives  130 us (28%)
  local copies, waits for them, and re-layouts  20.9 us (5%)
  other arithmetic  20.4 us (4%)
  between operations  14.9 us (3%)
  matrix products  7.98 us (2%)
    unnamed x5, waiting for transfers between devices  268 us
    all_gather x1, blocking collectives, on_device(): lax.all_gather(normed, ('seq', 'tp'), axis=0, tiled=True)  55.1 us
    all_gather x1, blocking collectives, on_device(): lax.all_gather(normed_mid, ('seq', 'tp'), axis=0, tiled=True)  48 us
    all_gather x2, blocking collectives, joined(): everything = jax.tree.map(lambda part: lax.all_gather(part, axis), value)  27.1 us
  transfers between devices with their start and end apart: 3, of which 2 were waited for; matrix products, arithmetic and copies ran while one was open for 1% of the time, Pallas kernels for 0%

commit v1 on v0

--- a/solution.py
+++ b/solution.py
@@ -209,7 +209,10 @@
     qkv_width = w_qkv.shape[2]
     flat_qkv = w_qkv.reshape(w_qkv.shape[0], 3 * qkv_width)
     projected = jnp.dot(
-        lax.all_gather(normed, ("seq", "tp"), axis=0, tiled=True),
+        jnp.concatenate(
+            lax.all_to_all(jnp.stack([normed] * lax.axis_size(("seq", "tp"))), ("seq", "tp"), 0, 0),
+            axis=0,
+        ),
         flat_qkv,
         preferred_element_type=jnp.float32,
     )

time: 464 us -> 435 us (0.938)
  blocking collectives: 130 us -> 75.2 us
  starting transfers between devices: 0.09 us -> 13.9 us
  waiting for transfers between devices: 268 us -> 278 us
  local copies, waits for them, and re-layouts: 20.9 us -> 26.2 us
    all_gather x1 -> x0, blocking collectives: 55.1 us -> none  [on_device(): lax.all_gather(normed, ('seq', 'tp'), axis=0, tiled=True)]
    all_to_all x0 -> x1, starting transfers between devices: none -> 13.8 us  [on_device(): lax.all_to_all(jnp.stack([normed] * lax.axis_size(('seq', 'tp'))), ('seq'...]
    all_to_all x0 -> x1, waiting for transfers between devices: none -> 10.1 us  [on_device(): lax.all_to_all(jnp.stack([normed] * lax.axis_size(('seq', 'tp'))), ('seq'...]
  transfers between devices with their start and end apart: 3 -> 4, of which waited for: 2 -> 3; matrix products, arithmetic and copies ran while one was open for 1% -> 3% of each run, Pallas kernels for 0% -> 0%
where the time goes in v1:
time: 435 us; the launch traced here: 434 us
  waiting for transfers between devices  278 us (64%)
  blocking collectives  75.2 us (17%)
  local copies, waits for them, and re-layouts  26.2 us (6%)
  other arithmetic  16.2 us (4%)
  between operations  14.9 us (3%)
  starting transfers between devices  13.9 us (3%)
  matrix products  9.99 us (2%)
    unnamed x5, waiting for transfers between devices  268 us
    all_gather x1, blocking collectives, on_device(): lax.all_gather(normed_mid, ('seq', 'tp'), axis=0, tiled=True)  48 us
    all_gather x2, blocking collectives, joined(): everything = jax.tree.map(lambda part: lax.all_gather(part, axis), value)  27.2 us
    all_to_all x1, starting transfers between devices, on_device(): lax.all_to_all(jnp.stack([normed] * lax.axis_size(('seq', 'tp'))), ('seq'...  13.8 us
    all_to_all x1, waiting for transfers between devices, on_device(): lax.all_to_all(jnp.stack([normed] * lax.axis_size(('seq', 'tp'))), ('seq'...  10.1 us
  transfers between devices with their start and end apart: 4, of which 3 were waited for; matrix products, arithmetic and copies ran while one was open for 3% of the time, Pallas kernels for 0%

profile of v1, /device:TPU:8, one launch (start us, length us, event | category | flops | bytes accessed | tf_op | source)
XLA Modules:
  0.0 434.4 jit_solution(12755849233721052904)
XLA Ops:
  9.2 13.8 %all-to-all-start = ((bf16[64,4,1024]{2,1,0:T(4,128)(2,1)}), bf16[64,4,1024]{2,1,0:T(4,128)(2,1)S(1)}, u32[]{:S(2)}, u32[]{:S(2)}) async-start(bf16[64,4,1024]{2,1,0:T(4,128)(2,1)} %stack.2), calls=%async_computation | async-start | bytes 1048576 | tf_op jit(solution)/shard_map/all_to_all | solution.py:213
  25.0 1.7 copy.146
  26.7 2.6 copy.154
  31.0 10.1 %all-to-all-done = bf16[64,4,1024]{2,1,0:T(4,128)(2,1)S(1)} async-done(((bf16[64,4,1024]{2,1,0:T(4,128)(2,1)}), bf16[64,4,1024]{2,1,0:T(4,128)(2,1)S(1)}, u32[]{:S(2)}, u32[]{:S(2)}) %all-to-all-start) | async-done | bytes 524320 | tf_op jit(solution)/shard_map/all_to_all | solution.py:213
  41.9 1.5 fusion.10
  48.9 1.8 fusion.46
  51.0 1.2 fusion.20
  52.4 1.5 convolution_multiply_fusion.1
  53.9 1.0 fusion.22
  57.9 13.4 %all-gather = f32[512,2,4]{2,1,0:T(2,128)S(1)} all-gather(f32[64,2,4]{2,1,0:T(2,128)S(1)} %copy.150), channel_id=2, replica_groups=mesh['req'=8,'seq'=8,'tp'=8] {'seq'}, dimensions={0}, use_global_device_ids=true | all-gather | bytes 18432 | tf_op jit(solution)/shard_map/all_gather | solution.py:13
  71.6 13.7 %all-gather.1 = f32[512,2,4]{2,1,0:T(2,128)S(1)} all-gather(f32[64,2,4]{2,1,0:T(2,128)S(1)} %copy.153), channel_id=3, replica_groups=mesh['req'=8,'seq'=8,'tp'=8] {'seq'}, dimensions={0}, use_global_device_ids=true | all-gather | bytes 18432 | tf_op jit(solution)/shard_map/all_gather | solution.py:13
  87.0 14.4 %while.19 = (s32[]{:T(128)}, f32[64,2,4]{0,2,1:T(4,128)S(1)}, f32[64,2,4]{0,2,1:T(4,128)S(1)}, f32[64,2,4,64]{3,2,1,0:T(4,128)S(1)}, f32[8,64,2,4]{1,3,2,0:T(4,1...) while((s32[]{:T(128)}, f32[64,2,4]{0,2,1:T(4,128)S(1)}, ...), condition=%wide.region_10.11_spmd, body=%wide.region_9.10_spmd.sunk | while | flops 101381 | bytes 684175 | solution.py:19
  87.3 1.0 constant_dynamic-slice_fusion.2
  91.4 1.0 constant_dynamic-slice_fusion.2
  93.5 1.0 constant_dynamic-slice_fusion.2
  97.6 1.0 constant_dynamic-slice_fusion.2
  99.6 1.0 constant_dynamic-slice_fusion.2
  103.5 1.3 dynamic-slice
  105.4 73.2 %all-reduce.5.cloned.1.call-done = bf16[32,1024]{1,0:T(8,128)(2,1)} async-done(((bf16[32,1024]{1,0:T(8,128)(2,1)}), bf16[32,1024]{1,0:T(8,128)(2,1)}) %all-reduce.5.cloned.1.call-update) | async-done | bytes 65552
  180.2 48.0 %all-gather.3 = bf16[64,4,1024]{2,1,0:T(4,128)(2,1)S(1)} all-gather(bf16[1,4,1024]{2,1,0:T(4,128)(2,1)S(1)} %fusion.38), channel_id=1, replica_groups=mesh['req'=8,'seq'=8,'tp'=8] {'seq','tp'}, dimensions={0}, use_global_device_ids=true | all-gather | bytes 532480 | tf_op jit(solution)/shard_map/all_gather | solution.py:262
  228.7 1.4 fusion.13
  230.1 1.3 dynamic-slice.2
  232.0 194.5 %all-reduce.7.cloned.1.call-done = f32[256,1024]{1,0:T(8,128)} async-done(((f32[256,1024]{1,0:T(8,128)}), f32[256,1024]{1,0:T(8,128)}) %all-reduce.7.cloned.1.call-update) | async-done | bytes 1048592
  426.5 1.4 fusion.34
  (150 shorter events, 31.1 us)
Async XLA Ops:
  6.5 96.1 %copy-start = (bf16[128,1024]{1,0:T(8,128)(2,1)S(1)}, bf16[128,1024]{1,0:T(8,128)(2,1)}, u32[]{:S(2)}) copy-start(bf16[128,1024]{1,0:T(8,128)(2,1)} %param.18) | copy-start | bytes 786436
  6.5 16.5 %copy-start.13 = (s32[64,64]{1,0:T(8,128)S(1)}, s32[64,64]{1,0:T(8,128)}, u32[]{:S(2)}) copy-start(s32[64,64]{1,0:T(8,128)} %param.28) | copy-start | bytes 49156
  6.5 17.7 %copy-start.19 = (s32[64]{0:T(128)S(1)}, s32[64]{0:T(128)}, u32[]{:S(2)}) copy-start(s32[64]{0:T(128)} %param.29) | copy-start | bytes 772
  6.5 17.8 %copy-start.15 = (s32[64,4]{0,1:T(4,128)S(1)}, s32[64,4]{0,1:T(4,128)}, u32[]{:S(2)}) copy-start(s32[64,4]{0,1:T(4,128)} %param.27) | copy-start | bytes 3076
  6.5 18.1 %copy-start.3 = (bf16[1024,3,128]{2,0,1:T(8,128)(2,1)S(1)}, bf16[1024,3,128]{2,0,1:T(8,128)(2,1)}, u32[]{:S(2)}) copy-start(bf16[1024,3,128]{2,0,1:T(8,128)(2,1)} %param.17) | copy-start | bytes 2359300
  9.2 31.8 %all-to-all-start = ((bf16[64,4,1024]{2,1,0:T(4,128)(2,1)}), bf16[64,4,1024]{2,1,0:T(4,128)(2,1)S(1)}, u32[]{:S(2)}, u32[]{:S(2)}) async-start(bf16[64,4,1024]{2,1,0:T(4,128)(2,1)} %stack.2), calls=%async_computation | async-start | bytes 1048576 | tf_op jit(solution)/shard_map/all_to_all | solution.py:213
  23.0 62.8 %all-gather.6.cloned.1.call-start = ((), (), s32[]{:S(2)}) async-start(), calls=%async_computation.1 | async-start | bytes 2359296 | tf_op jit(solution)/shard_map/all_gather | solution.py:13
  26.7 2.7 copy-start.20
  26.7 3.4 copy-start.14
  43.4 0.7 copy-start.2
  44.8 0.6 copy-start.6
  44.8 7.5 %copy-start.1 = (bf16[24,256,128]{1,2,0:T(8,128)(2,1)S(1)}, bf16[24,256,128]{1,2,0:T(8,128)(2,1)}, u32[]{:S(2)}) copy-start(bf16[24,256,128]{1,2,0:T(8,128)(2,1)} %copy.154) | copy-start | bytes 4718596
  52.4 3.6 copy-start.7
  52.4 3.7 copy-start.5
  52.4 4.1 copy-start.11
  52.4 4.2 copy-start.10
  55.0 123.6 %all-reduce.5.cloned.1.call-start = ((), (), s32[]{:S(2)}) async-start(), calls=%async_computation.2 | async-start | bytes 131072
  57.4 28.2 %copy-start.16 = (f32[2]{0:T(128)S(1)}, f32[2]{0:T(128)}, u32[]{:S(2)}) copy-start(f32[2]{0:T(128)} %get-tuple-element.257) | copy-start | bytes 28
  57.5 28.2 %copy-start.17 = (f32[2]{0:T(128)S(1)}, f32[2]{0:T(128)}, u32[]{:S(2)}) copy-start(f32[2]{0:T(128)} %get-tuple-element.258) | copy-start | bytes 28
  102.0 76.6 %copy-start.9 = (bf16[4,1024]{1,0:T(4,128)(2,1)S(1)}, bf16[4,1024]{1,0:T(4,128)(2,1)}, u32[]{:S(2)}) copy-start(bf16[4,1024]{1,0:T(4,128)(2,1)} %param.16) | copy-start | bytes 24580
  102.0 77.5 %copy-start.18 = (f32[1024]{0:T(1024)S(1)}, f32[1024]{0:T(1024)}, u32[]{:S(2)}) copy-start(f32[1024]{0:T(1024)} %param.21) | copy-start | bytes 12292
  102.4 126.0 %copy-start.8 = (bf16[1024,1,128]{2,0,1:T(8,128)(2,1)S(1)}, bf16[1024,1,128]{2,0,1:T(8,128)(2,1)}, u32[]{:S(2)}) copy-start(bf16[1024,1,128]{2,0,1:T(8,128)(2,1)} %param.22) | copy-start | bytes 786436
  102.5 126.2 %copy-start.12 = (bf16[1,64,1024]{2,1,0:T(8,128)(2,1)S(1)}, bf16[1,64,1024]{2,1,0:T(8,128)(2,1)}, u32[]{:S(2)}) copy-start(bf16[1,64,1024]{2,1,0:T(8,128)(2,1)} %param.23) | copy-start | bytes 393220
  103.4 323.1 %all-reduce.7.cloned.1.call-start = ((), (), s32[]{:S(2)}) async-start(), calls=%async_computation.3 | async-start | bytes 2097152
  (1 other events, 0.6 us)
Sparse Core Ops, SparseCore 0:
  55.1 27.3 all-gather.5
  103.5 74.9 all-reduce.4
  230.2 196.2 all-reduce.6
